TPU v7x, 32 devices: a whole 2x2x4 slice. The times are simulated.
32 devices in a mesh: seq: 4 (over y, x), dp: 8 (over z, core).
Axes of the slice: x: 2, y: 2, z: 4, core: 2. Of those that a mesh axis runs over, the one named last changes fastest.
Arguments:
- layer_input: bfloat16 [8, 1024, 8192], P('dp', 'seq'), may hold values from -400 to 400
- frozen_queries: bfloat16 [8, 1024, 6144], P('dp', 'seq'), may hold values from -70 to 70
- frozen_keys: bfloat16 [8, 1024, 768], P('dp', 'seq'), may hold values from -6 to 6
- frozen_values: bfloat16 [8, 1024, 768], P('dp', 'seq'), may hold values from -6 to 6
- output_gradient: bfloat16 [8, 1024, 6144], P('dp', 'seq'), may hold values from -6 to 6
- norm_scale_vector: bfloat16 [8192], replicated, may hold values from 0.5 to 1.5
- query_down_weight: bfloat16 [8, 8192], replicated, may hold values from -0.0625 to 0.0625
- query_up_weight: bfloat16 [8, 6144], replicated, may hold values from -2 to 2
- value_down_weight: bfloat16 [8, 8192], replicated, may hold values from -0.0625 to 0.0625
- value_up_weight: bfloat16 [8, 768], replicated, may hold values from -2 to 2
- head_ordering: int32 [6], replicated, may hold values from 0 to 5, each once
Outputs:
- grad_query_a: float32 [8, 8192], replicated
- grad_query_b: float32 [8, 6144], replicated
- grad_value_a: float32 [8, 8192], replicated
- grad_value_b: float32 [8, 768], replicated
- grad_gain: float32 [8192], replicated
Inputs may be any that keep to these rules, and one draw needn't show every extreme that they name: `head_ordering`: a permutation of the 6 key-value heads.
All inputs are finite; a program needn't handle non-finite values.
Results may differ from a plain program's by a relative error of at most 0.012.
The roundings to bfloat16 on the way count: a program that leaves them out, or rounds other values in their place, can miss the bound.
Values may be sent and summed in bfloat16 or wider, within the bound.
A program may use at most 128 MiB of HBM per device.

v0:
```python
import functools
import math

import jax
import jax.numpy as jnp
from jax import lax
from jax.experimental import pallas as pl
from jax.experimental.pallas import tpu as pltpu
from jax.sharding import PartitionSpec as P

HEAD_SIZE = 128
CORES = 2
LANES = 128
TOGETHER = 8


EPS = 1e-05
ADAPTER_SCALE = 2.0
F32 = jnp.float32
BF16 = jnp.bfloat16
NT = (((1,), (1,)), ((), ()))
NN = (((1,), (0,)), ((), ()))


def from_behind(block, axis, distance):
    devices = range(lax.axis_size(axis))
    route = [((i - distance) % len(devices), i) for i in devices]
    return lax.ppermute(block, axis, route)


def dot(left, right, dims):
    return lax.dot_general(left, right, dims, preferred_element_type=F32)


def pick(order, slot):
    count = order.shape[0]
    shift = lax.rem(lax.axis_index("seq"), 2) * (count // 2)
    return order[lax.rem(slot + shift, count)]


def scaled(block, scale_ref, first, chunks):
    scale = scale_ref[pl.ds(first, chunks), :].astype(F32)
    return jnp.concatenate(
        [
            (block[:, i * LANES : (i + 1) * LANES] * scale[i : i + 1]).astype(BF16)
            for i in range(chunks)
        ],
        axis=1,
    )


def flipped(columns, start, count):
    rows = lax.broadcasted_iota(jnp.int32, (count, columns.shape[1]), 0)
    cols = lax.broadcasted_iota(jnp.int32, (count, columns.shape[1]), 1)
    pick = jnp.where(rows + start == cols, ADAPTER_SCALE, 0.0).astype(BF16)
    return dot(pick, columns, NT).astype(BF16)


def prologue_kernel(
    heads_ref,
    x_ref,
    scale_ref,
    qdown_ref,
    vdown_ref,
    fv_ref,
    vup_ref,
    inv_ref,
    qmid_ref,
    vmid_ref,
    value_ref,
    given_ref,
):
    width = x_ref.shape[1]
    hidden = x_ref[...].astype(F32)
    inverse = lax.rsqrt(jnp.sum(hidden * hidden, axis=-1, keepdims=True) * (1.0 / width) + EPS)
    inv_ref[...] = inverse
    normed = scaled(hidden * inverse, scale_ref, 0, width // LANES)
    qmid_ref[...] = dot(normed, qdown_ref[...], NT).astype(BF16)
    value_mid = dot(normed, vdown_ref[...], NT).astype(BF16)
    vmid_ref[...] = value_mid
    value_ref[...] = (
        fv_ref[...].astype(F32) + dot((value_mid * ADAPTER_SCALE).astype(BF16), vup_ref[...], NN)
    ).astype(BF16)
    half = given_ref.shape[1] // HEAD_SIZE
    for i in range(half):
        at = pl.multiple_of(pick(heads_ref, half + i) * HEAD_SIZE, HEAD_SIZE)
        given_ref[:, i * HEAD_SIZE : (i + 1) * HEAD_SIZE] = value_ref[:, pl.ds(at, HEAD_SIZE)]


def prologue(heads, x, scale, qdown, vdown, frozen_values, vup, steps):
    rows, width = x.shape
    block = rows // steps
    kv = frozen_values.shape[1]
    rank = qdown.shape[0]
    whole = lambda i, heads: (0, 0)
    by_rows = lambda i, heads: (i, 0)
    return pl.pallas_call(
        prologue_kernel,
        grid_spec=pltpu.PrefetchScalarGridSpec(
            num_scalar_prefetch=1,
            grid=(steps,),
            in_specs=[
                pl.BlockSpec((block, width), by_rows),
                pl.BlockSpec(scale.shape, whole),
                pl.BlockSpec(qdown.shape, whole),
                pl.BlockSpec(vdown.shape, whole),
                pl.BlockSpec((block, kv), by_rows),
                pl.BlockSpec(vup.shape, whole),
            ],
            out_specs=[
                pl.BlockSpec((block, 1), by_rows),
                pl.BlockSpec((block, rank), by_rows),
                pl.BlockSpec((block, rank), by_rows),
                pl.BlockSpec((block, kv), by_rows),
                pl.BlockSpec((block, kv // 2), by_rows),
            ],
        ),
        out_shape=[
            jax.ShapeDtypeStruct((rows, 1), F32),
            jax.ShapeDtypeStruct((rows, rank), BF16),
            jax.ShapeDtypeStruct((rows, rank), BF16),
            jax.ShapeDtypeStruct((rows, kv), BF16),
            jax.ShapeDtypeStruct((rows, kv // 2), BF16),
        ],
        cost_estimate=pl.CostEstimate(
            flops=40 * rows * width, bytes_accessed=2 * rows * width, transcendentals=0
        ),
        name="prologue",
    )(heads, x, scale, qdown, vdown, frozen_values, vup)


def attention_kernel(has_start, with_prior, heads_ref, *refs):
    refs = list(refs)
    fq_ref, grad_ref, key_ref, value_ref, mid_ref, up_ref = refs[:6]
    refs = refs[6:]
    if has_start:
        start_ref = refs.pop(0)
    if with_prior:
        prior_key_ref, prior_value_ref = refs.pop(0), refs.pop(0)
    dv_ref, qb_ref, dq_mid_ref = refs[:3]
    rows = fq_ref.shape[0]
    heads = fq_ref.shape[1] // HEAD_SIZE
    rank = up_ref.shape[0]
    factor = 1.0 / math.sqrt(HEAD_SIZE)

    @pl.when(pl.program_id(0) == 0)
    def _():
        dq_mid_ref[...] = start_ref[...] if has_start else jnp.zeros_like(dq_mid_ref)

    keys = key_ref[...]
    values = value_ref[...]
    if with_prior:
        keys = jnp.concatenate([keys, prior_key_ref[...]], axis=0)
        values = jnp.concatenate([values, prior_value_ref[...]], axis=0)
    keys_t = keys.T
    query_mid = (mid_ref[...] * ADAPTER_SCALE).astype(BF16)
    mid_t = flipped(mid_ref[...], 0, rank)
    key_pos = lax.broadcasted_iota(jnp.int32, (rows, rows), 0)
    query_pos = lax.broadcasted_iota(jnp.int32, (rows, rows), 1)
    causal = key_pos <= query_pos
    together = math.gcd(heads, TOGETHER)
    up = up_ref[...]
    query = (fq_ref[...].astype(F32) + dot(query_mid, up, NN)).astype(BF16)
    dv = None
    dqueries = []
    for j in range(0, heads, together):
        stacked = lambda array: jnp.concatenate(
            [array[:, i * HEAD_SIZE : (i + 1) * HEAD_SIZE] for i in range(j, j + together)], axis=0
        )
        grad = stacked(grad_ref)
        scores = dot(keys, stacked(query), NT)
        own = jnp.concatenate(
            [
                jnp.where(causal, scores[:rows, i * rows : (i + 1) * rows], -jnp.inf)
                for i in range(together)
            ],
            axis=1,
        )
        scores = jnp.concatenate([own, scores[rows:]], axis=0) if with_prior else own
        top = jnp.max(scores, axis=0, keepdims=True)
        exponent = jnp.exp2((scores - top) * (factor * math.log2(math.e)))
        probs = exponent * (1.0 / jnp.sum(exponent, axis=0, keepdims=True))
        weights = probs.astype(BF16)
        dprob = dot(values, grad, NT)
        delta = jnp.sum(weights.astype(F32) * dprob, axis=0, keepdims=True)
        dscore = (probs * (dprob - delta)).astype(BF16)
        term = dot(weights, grad, NN)
        dv = term if dv is None else dv + term
        dquery = (dot(keys_t, dscore, NN) * factor).astype(BF16)
        dqueries += [dquery[:, i * rows : (i + 1) * rows] for i in range(together)]
    dquery = jnp.concatenate(dqueries, axis=0)
    qb_ref[...] = dot(mid_t, dquery, NT)
    dq_mid_ref[...] += dot(up, dquery, NN)
    dv_ref[...] = dv[:rows]
    if with_prior:
        refs[3][...] = dv[rows:].astype(BF16)


def attention(first, count, heads, fq, grads, keys, values, mid, up, start, prior):
    rows, queries = fq.shape
    kv_heads = keys.shape[1] // HEAD_SIZE
    wide = queries // kv_heads
    rank = up.shape[0]
    by_head = lambda i, heads: (0, pick(heads, first + i))
    by_slot = lambda i, heads: (0, i)
    whole = lambda i, heads: (0, 0)
    narrow = pl.BlockSpec((rows, HEAD_SIZE), by_head)
    broad = pl.BlockSpec((rows, wide), by_head)
    slot = pl.BlockSpec((rows, HEAD_SIZE), by_slot)
    operands = [fq, grads, keys, values, mid, up]
    in_specs = [
        broad,
        broad,
        narrow,
        narrow,
        pl.BlockSpec(mid.shape, whole),
        pl.BlockSpec((rank, wide), by_head),
    ]
    out_specs = [
        slot,
        pl.BlockSpec((rank, wide), by_slot),
        pl.BlockSpec((rank, rows), whole),
    ]
    out_shape = [
        jax.ShapeDtypeStruct((rows, count * HEAD_SIZE), F32),
        jax.ShapeDtypeStruct((rank, count * wide), F32),
        jax.ShapeDtypeStruct((rank, rows), F32),
    ]
    if start is not None:
        operands.append(start)
        in_specs.append(pl.BlockSpec(start.shape, whole))
    if prior is not None:
        operands += list(prior)
        in_specs += [narrow, slot]
        out_specs.append(slot)
        out_shape.append(jax.ShapeDtypeStruct((rows, count * HEAD_SIZE), BF16))
    return pl.pallas_call(
        functools.partial(attention_kernel, start is not None, prior is not None),
        grid_spec=pltpu.PrefetchScalarGridSpec(
            num_scalar_prefetch=1, grid=(count,), in_specs=in_specs, out_specs=out_specs
        ),
        out_shape=out_shape,
        cost_estimate=pl.CostEstimate(
            flops=count * 24 * rows * rows * wide,
            bytes_accessed=count * 4 * rows * wide,
            transcendentals=0,
        ),
        name="attention",
    )(heads, *operands)


def epilogue_kernel(
    counts,
    heads_ref,
    x_ref,
    inv_ref,
    scale_ref,
    qdown_ref,
    vdown_ref,
    dq_mid_ref,
    handed_ref,
    vup_ref,
    vmid_ref,
    *refs,
):
    dv_refs, qb_refs = refs[: len(counts)], refs[len(counts) : 2 * len(counts)]
    packed_ref, inner_ref, gain_ref = refs[2 * len(counts) :]
    step = pl.program_id(0)
    block = x_ref.shape[1]
    rank = vup_ref.shape[0]
    full = gain_ref.shape[0] * block
    kv = vup_ref.shape[1]
    half = handed_ref.shape[1] // HEAD_SIZE
    wide = qb_refs[0].shape[1] // counts[0][1]
    queries = kv // HEAD_SIZE * wide
    base = 2 * full + queries

    @pl.when(step == 0)
    def _():
        mid_t = flipped(vmid_ref[...], 0, rank)
        dv_mid = jnp.zeros(dq_mid_ref.shape, F32)
        for (first, count), dv_ref, qb_ref in zip(counts, dv_refs, qb_refs):
            for i in range(count):
                cols = slice(i * HEAD_SIZE, (i + 1) * HEAD_SIZE)
                dv = dv_ref[:, cols]
                if first + i >= half:
                    given = first + i - half
                    other = handed_ref[:, given * HEAD_SIZE : (given + 1) * HEAD_SIZE]
                    dv = dv + other.astype(F32)
                dv = dv.astype(BF16)
                head = pick(heads_ref, first + i)
                at = pl.multiple_of(head * HEAD_SIZE, HEAD_SIZE)
                dv_mid = dv_mid + dot(vup_ref[:, pl.ds(at, HEAD_SIZE)], dv, NT)
                at = pl.multiple_of(base + head * HEAD_SIZE, HEAD_SIZE)
                packed_ref[:, pl.ds(at, HEAD_SIZE)] = dot(mid_t, dv, NN).astype(BF16)
                at = pl.multiple_of(2 * full + head * wide, HEAD_SIZE)
                packed_ref[:, pl.ds(at, wide)] = qb_ref[:, i * wide : (i + 1) * wide].astype(BF16)
        inner_ref[...] = (
            ADAPTER_SCALE * jnp.concatenate([dq_mid_ref[...], dv_mid], axis=0)
        ).astype(BF16)
        gain_ref[...] = jnp.zeros_like(gain_ref)
        used = base + kv + block
        if used < packed_ref.shape[1]:
            packed_ref[:, used:] = jnp.zeros((rank, packed_ref.shape[1] - used), BF16)

    inner = inner_ref[...]
    unit = x_ref[...].astype(F32) * inv_ref[...]
    normed = scaled(unit, scale_ref, 0, block // LANES)
    raw = dot(inner, normed, NN).astype(BF16)
    at = pl.multiple_of(step * block, block)
    packed_ref[:, pl.ds(at, block)] = raw[:rank]
    packed_ref[:, pl.ds(at + full, block)] = raw[rank:]
    spread = dot(inner, unit.astype(BF16), NN)
    gain = jnp.sum(
        qdown_ref[...].astype(F32) * spread[:rank] + vdown_ref[...].astype(F32) * spread[rank:],
        axis=0,
        keepdims=True,
    )
    row = lax.broadcasted_iota(jnp.int32, gain_ref.shape, 0)
    gain_ref[...] = jnp.where(row == step, gain, gain_ref[...])

    @pl.when(step == pl.num_programs(0) - 1)
    def _():
        packed_ref[:, base + kv : base + kv + block] = gain_ref[...].astype(BF16)


def epilogue(heads, counts, x, inverse, scale, qdown, vdown, dq_mid, handed, vup, vmid, dvs, qbs, total):
    rows, width = x.shape
    rank = vup.shape[0]
    block = width // rank
    whole = lambda j, heads: (0, 0)
    by_cols = lambda j, heads: (0, j)
    kept = lambda a: pl.BlockSpec(a.shape, whole)
    return pl.pallas_call(
        functools.partial(epilogue_kernel, counts),
        grid_spec=pltpu.PrefetchScalarGridSpec(
            num_scalar_prefetch=1,
            grid=(rank,),
            in_specs=[
                pl.BlockSpec((rows, block), by_cols),
                kept(inverse),
                pl.BlockSpec((block // LANES, LANES), lambda j, heads: (j, 0)),
                pl.BlockSpec((rank, block), by_cols),
                pl.BlockSpec((rank, block), by_cols),
                kept(dq_mid),
                kept(handed),
                kept(vup),
                kept(vmid),
            ]
            + [kept(a) for a in (*dvs, *qbs)],
            out_specs=pl.BlockSpec((rank, total), whole),
            scratch_shapes=[
                pltpu.VMEM((2 * rank, rows), BF16),
                pltpu.VMEM((rank, block), F32),
            ],
        ),
        out_shape=jax.ShapeDtypeStruct((rank, total), BF16),
        cost_estimate=pl.CostEstimate(
            flops=80 * rows * width, bytes_accessed=2 * rows * width, transcendentals=0
        ),
        name="epilogue",
    )(heads, x, inverse, scale, qdown, vdown, dq_mid, handed, vup, vmid, *dvs, *qbs)


def finish_kernel(limit, full_ref, qa_ref, qb_ref, va_ref, vb_ref, gain_ref):
    sums = full_ref[...].astype(F32)
    squares = jnp.sum(jnp.sum(sums * sums, axis=1, keepdims=True), axis=0, keepdims=True)
    scale = jnp.minimum(1.0, limit / jnp.sqrt(squares))
    at = 0
    for out in (qa_ref, va_ref, qb_ref, vb_ref):
        out[...] = full_ref[:, at : at + out.shape[1]].astype(F32) * scale
        at += out.shape[1]
    rank = full_ref.shape[0]
    chunks = gain_ref.shape[0] // rank
    for c in range(chunks):
        piece = full_ref[:, at + c * LANES : at + (c + 1) * LANES].astype(F32) * scale
        gain_ref[pl.ds(c, rank, stride=chunks), :] = piece


def finished(full, limit, widths, width):
    rank = full.shape[0]
    vmem = pl.BlockSpec(memory_space=pltpu.VMEM)
    return pl.pallas_call(
        functools.partial(finish_kernel, limit),
        in_specs=[vmem],
        out_specs=[vmem] * (len(widths) + 1),
        out_shape=[jax.ShapeDtypeStruct((rank, w), F32) for w in widths]
        + [jax.ShapeDtypeStruct((width // LANES, LANES), F32)],
        name="finished",
    )(full)


def reduce_kernel(
    seqs,
    planes,
    packed_ref,
    full,
    parts,
    column,
    send_one,
    recv_one,
    send_two,
    recv_two,
    send_three,
    recv_three,
):
    group = seqs * CORES
    piece = full.shape[1] // group
    place = lax.axis_index("dp")
    plane = place // CORES
    me = lax.axis_index("seq") * CORES + place % CORES

    def in_group(k):
        peer = lax.rem(me + k, group)
        return peer, {"seq": peer // CORES, "dp": plane * CORES + peer % CORES}

    def in_column(k):
        return {"dp": lax.rem(plane + k, planes) * CORES + place % CORES}

    def span(index):
        return pl.ds(pl.multiple_of(index * piece, piece), piece)

    barrier = pltpu.get_barrier_semaphore()
    for k in range(1, group):
        pl.semaphore_signal(
            barrier, inc=1, device_id=in_group(k)[1], device_id_type=pl.DeviceIdType.MESH
        )
    for k in range(1, planes):
        pl.semaphore_signal(
            barrier, inc=1, device_id=in_column(k), device_id_type=pl.DeviceIdType.MESH
        )
    pl.semaphore_wait(barrier, group + planes - 2)

    def remote(source, target, send, recv, device):
        copy = pltpu.make_async_remote_copy(
            src_ref=source,
            dst_ref=target,
            send_sem=send,
            recv_sem=recv,
            device_id=device,
            device_id_type=pl.DeviceIdType.MESH,
        )
        copy.start()
        return copy

    first = []
    for k in range(1, group):
        peer, device = in_group(k)
        first.append(
            remote(
                packed_ref.at[:, span(peer)],
                parts.at[k - 1],
                send_one.at[k - 1],
                recv_one.at[k - 1],
                device,
            )
        )
    total = packed_ref[:, span(me)].astype(F32)
    for k in range(1, group):
        first[k - 1].wait_recv()
        total = total + parts[k - 1].astype(F32)
    column[plane] = total.astype(BF16)
    second = [
        remote(
            column.at[plane],
            column.at[plane],
            send_two.at[k - 1],
            recv_two.at[k - 1],
            in_column(k),
        )
        for k in range(1, planes)
    ]
    for copy in second:
        copy.wait_recv()
    total = column[0].astype(F32)
    for i in range(1, planes):
        total = total + column[i].astype(F32)
    full[:, span(me)] = total.astype(BF16)
    third = [
        remote(
            full.at[:, span(me)],
            full.at[:, span(me)],
            send_three.at[k - 1],
            recv_three.at[k - 1],
            in_group(k)[1],
        )
        for k in range(1, group)
    ]
    for copy in third:
        copy.wait_recv()
    for copy in first + second + third:
        copy.wait_send()


def reduced(packed, seqs, planes):
    rank, total = packed.shape
    group = seqs * CORES
    piece = total // group
    vmem = pl.BlockSpec(memory_space=pltpu.VMEM)
    dma = pltpu.SemaphoreType.DMA
    return pl.pallas_call(
        functools.partial(reduce_kernel, seqs, planes),
        in_specs=[vmem],
        out_specs=vmem,
        out_shape=jax.ShapeDtypeStruct((rank, total), BF16),
        scratch_shapes=[
            pltpu.VMEM((group - 1, rank, piece), BF16),
            pltpu.VMEM((planes, rank, piece), BF16),
            dma((group - 1,)),
            dma((group - 1,)),
            dma((max(planes - 1, 1),)),
            dma((max(planes - 1, 1),)),
            dma((group - 1,)),
            dma((group - 1,)),
        ],
        compiler_params=pltpu.CompilerParams(collective_id=0, has_side_effects=True),
        name="reduced",
    )(packed)


def shards(
    layer_input,
    frozen_queries,
    frozen_keys,
    frozen_values,
    output_gradient,
    norm_scale_vector,
    query_down_weight,
    query_up_weight,
    value_down_weight,
    value_up_weight,
    head_ordering,
):
    seqs = lax.axis_size("seq")
    planes = lax.axis_size("dp") // CORES
    rank, width = query_down_weight.shape
    queries = query_up_weight.shape[1]
    kv = value_up_weight.shape[1]
    half = head_ordering.shape[0] // 2
    heads = head_ordering
    scale = norm_scale_vector.reshape(width // LANES, LANES)
    x, fq, grads, keys = layer_input[0], frozen_queries[0], output_gradient[0], frozen_keys[0]
    prior_keys = from_behind(keys, "seq", 1)
    inverse, qmid, vmid, values, given = prologue(
        heads, x, scale, query_down_weight, value_down_weight, frozen_values[0], value_up_weight, 4
    )
    prior_values = from_behind(given, "seq", 1)
    counts = ((half, half - 1), (0, half), (2 * half - 1, 1))
    attend = functools.partial(attention, heads=heads, fq=fq, grads=grads, keys=keys)
    attend = functools.partial(attend, values=values, mid=qmid, up=query_up_weight)
    dv_a, qb_a, dq_mid = attend(*counts[0], start=None, prior=None)
    dv_b, qb_b, dq_mid, dv_prior = attend(
        *counts[1], start=dq_mid, prior=(prior_keys, prior_values)
    )
    handed = from_behind(dv_prior, "seq", -1)
    dv_c, qb_c, dq_mid = attend(*counts[2], start=dq_mid, prior=None)
    used = 2 * width + queries + kv + width // rank
    unit = seqs * CORES * LANES
    total = -(-used // unit) * unit
    packed = epilogue(
        heads,
        counts,
        x,
        inverse,
        scale,
        query_down_weight,
        value_down_weight,
        dq_mid,
        handed,
        value_up_weight,
        vmid,
        (dv_a, dv_b, dv_c),
        (qb_a, qb_b, qb_c),
        total,
    )
    limit = math.sqrt(rank * (2 * width + queries + kv) + width)
    qa, gqb, va, vb, gain = finished(
        reduced(packed, seqs, planes), limit, (width, queries, width, kv), width
    )
    return (qa, gqb, va, vb, gain.reshape(width))


def solution(mesh):
    placed = (
        P("dp", "seq", None),
        P("dp", "seq", None),
        P("dp", "seq", None),
        P("dp", "seq", None),
        P("dp", "seq", None),
        P(),
        P(),
        P(),
        P(),
        P(),
        P(),
    )
    return jax.shard_map(
        shards, mesh=mesh, in_specs=placed, out_specs=(P(), P(), P(), P(), P()), check_vma=False
    )
```

profile of v0, /device:TPU:0, one launch (start us, length us, event | category | flops | bytes accessed | tf_op | source)
XLA Modules:
  0.0 73.5 jit_solution(4246368556655571537)
XLA Ops:
  0.6 3.0 %collective-permute-start = (bf16[256,768]{1,0:T(8,128)(2,1)}, bf16[256,768]{1,0:T(8,128)(2,1)S(1)}, u32[]{:S(2)}, u32[]{:S(2)}) collective-permute-start(bf16[256,768]{1,0:T(8,128)(2,1)} %bitcast.16), channel_id=1, source_target_pairs={{24,0},{0,8},{8,16},{16,24},{25,1},{1,9},{9,17},{17,25},{26,2},{2,... | collective-permute-start | bytes 1179656 | tf_op jit(solution)/shard_map/ppermute | solution.py:28
  3.6 7.5 %prologue.1 = (f32[256,1]{1,0:T(8,128)}, bf16[256,8]{1,0:T(8,128)(2,1)}, bf16[256,8]{1,0:T(8,128)(2,1)}, bf16[256,768]{1,0:T(8,128)(2,1)}, bf16[256,384]{1,0:T(8,128)(2,1)}) custom-call(s32[6]{0:T(128)} %heads_ref.9, bf16[256,8192]{1,0:T(8,128)(2,1)} %bitcast.7, bf16[64,128]{1,0:T(8,128)(2,1)} %bitcast.20, bf16[8,8192]{1,0:T(8,128)(2,1)} %qdown_ref.3, ...), custom_call_target="tpu_custom_call" | custom-call | flops 83886080 | bytes 4194304 | tf_op jit(solution)/shard_map/prologue/pallas_call | solution.py:97
  11.1 1.5 %collective-permute-start.1 = (bf16[256,384]{1,0:T(8,128)(2,1)}, bf16[256,384]{1,0:T(8,128)(2,1)S(1)}, u32[]{:S(2)}, u32[]{:S(2)}) collective-permute-start(bf16[256,384]{1,0:T(8,128)(2,1)} %get-tuple-element.29), channel_id=1, source_target_pairs={{24,0},{0,8},{8,16},{16,24},{25,1},{1,9},{9,17},{17,25},{26,2},{2,... | collective-permute-start | bytes 589832 | tf_op jit(solution)/shard_map/ppermute | solution.py:28
  12.6 6.6 %attention.3 = (f32[256,256]{1,0:T(8,128)}, f32[8,2048]{1,0:T(8,128)}, f32[8,256]{1,0:T(8,128)}) custom-call(s32[6]{0:T(128)} %heads_ref.9, bf16[256,6144]{1,0:T(8,128)(2,1)} %bitcast.9, bf16[256,6144]{1,0:T(8,128)(2,1)} %bitcast.12, bf16[256,768]{1,0:T(8,128)(2,1)} %bitcast.17, bf16[256,768]{1,0:T(8,128)(2,1)} %get-tuple-element.26.refs_3_, ...), custom_call_target="tpu_custom_call" | custom-call | flops 3221225472 | bytes 2097152 | tf_op jit(solution)/shard_map/attention/pallas_call | solution.py:237
  19.2 0.0 collective-permute-done.1.refs_8_
  19.3 0.0 copy-start.2
  19.3 0.0 collective-permute-done.refs_7_
  19.3 0.0 copy-start.1
  19.3 0.6 copy-done.2
  19.9 0.1 copy-done.1
  20.1 13.0 %attention.4 = (f32[256,384]{1,0:T(8,128)}, f32[8,3072]{1,0:T(8,128)}, f32[8,256]{1,0:T(8,128)}, bf16[256,384]{1,0:T(8,128)(2,1)}) custom-call(s32[6]{0:T(128)} %heads_ref.9, bf16[256,6144]{1,0:T(8,128)(2,1)} %bitcast.10, bf16[256,6144]{1,0:T(8,128)(2,1)} %bitcast.13, bf16[256,768]{1,0:T(8,128)(2,1)} %bitcast.18, ...), custom_call_target="tpu_custom_call" | custom-call | flops 4831838208 | bytes 3145728 | tf_op jit(solution)/shard_map/attention/pallas_call | solution.py:237
  33.1 1.5 %collective-permute-start.2 = (bf16[256,384]{1,0:T(8,128)(2,1)}, bf16[256,384]{1,0:T(8,128)(2,1)S(1)}, u32[]{:S(2)}, u32[]{:S(2)}) collective-permute-start(bf16[256,384]{1,0:T(8,128)(2,1)} %get-tuple-element.32), channel_id=1, source_target_pairs={{8,0},{16,8},{24,16},{0,24},{9,1},{17,9},{25,17},{1,25},{10,2},{18... | collective-permute-start | bytes 589832 | tf_op jit(solution)/shard_map/ppermute | solution.py:28
  34.5 4.5 %attention.5 = (f32[256,128]{1,0:T(8,128)}, f32[8,1024]{1,0:T(8,128)}, f32[8,256]{1,0:T(8,128)}) custom-call(s32[6]{0:T(128)} %heads_ref.9, bf16[256,6144]{1,0:T(8,128)(2,1)} %bitcast.11, bf16[256,6144]{1,0:T(8,128)(2,1)} %bitcast.14, bf16[256,768]{1,0:T(8,128)(2,1)} %bitcast.19, bf16[256,768]{1,0:T(8,128)(2,1)} %get-tuple-element.26.refs_3_, ...), custom_call_target="tpu_custom_call" | custom-call | flops 1610612736 | bytes 1048576 | tf_op jit(solution)/shard_map/attention/pallas_call | solution.py:237
  39.0 0.3 collective-permute-done.2.handed_ref
  39.3 0.0 copy-start
  39.4 0.7 copy-done
  40.0 8.7 %epilogue.1.packed_ref = bf16[8,24576]{1,0:T(8,128)(2,1)} custom-call(s32[6]{0:T(128)} %heads_ref.9, bf16[256,8192]{1,0:T(8,128)(2,1)} %bitcast.8, f32[256,1]{1,0:T(8,128)} %get-tuple-element.25.inv_ref, bf16[64,128]{1,0:T(8,128)(2,1)} %bitcast.21, bf16[8,8192]{1,0:T(8,128)(2,1)} %qdown_ref.3, bf16[8,8192]{1,0:T(8,128)(2,1)} %vdown_ref.3, ...), custom_call_target="tpu_custom_call" | custom-call | flops 167772160 | bytes 4194304 | tf_op jit(solution)/shard_map/epilogue/pallas_call | solution.py:334
  48.7 22.5 %reduced.1.full_ref = bf16[8,24576]{1,0:T(8,128)(2,1)} custom-call(bf16[8,24576]{1,0:T(8,128)(2,1)} %epilogue.1.packed_ref), custom_call_target="tpu_custom_call" | custom-call | tf_op jit(solution)/shard_map/reduced/pallas_call | solution.py:501
  71.3 2.2 %finished.1 = (f32[8,8192]{1,0:T(8,128)}, f32[8,6144]{1,0:T(8,128)}, f32[8,8192]{1,0:T(8,128)}, f32[8,768]{1,0:T(8,128)}, f32[64,128]{1,0:T(8,128)}) custom-call(bf16[8,24576]{1,0:T(8,128)(2,1)} %reduced.1.full_ref), custom_call_target="tpu_custom_call" | custom-call | tf_op jit(solution)/shard_map/finished/pallas_call | solution.py:383
Async XLA Ops:
  0.6 18.6 %collective-permute-start = (bf16[256,768]{1,0:T(8,128)(2,1)}, bf16[256,768]{1,0:T(8,128)(2,1)S(1)}, u32[]{:S(2)}, u32[]{:S(2)}) collective-permute-start(bf16[256,768]{1,0:T(8,128)(2,1)} %bitcast.16), channel_id=1, source_target_pairs={{24,0},{0,8},{8,16},{16,24},{25,1},{1,9},{9,17},{17,25},{26,2},{2,... | collective-permute-start | bytes 1179656 | tf_op jit(solution)/shard_map/ppermute | solution.py:28
  11.1 8.1 %collective-permute-start.1 = (bf16[256,384]{1,0:T(8,128)(2,1)}, bf16[256,384]{1,0:T(8,128)(2,1)S(1)}, u32[]{:S(2)}, u32[]{:S(2)}) collective-permute-start(bf16[256,384]{1,0:T(8,128)(2,1)} %get-tuple-element.29), channel_id=1, source_target_pairs={{24,0},{0,8},{8,16},{16,24},{25,1},{1,9},{9,17},{17,25},{26,2},{2,... | collective-permute-start | bytes 589832 | tf_op jit(solution)/shard_map/ppermute | solution.py:28
  19.3 0.7 copy-start.2
  19.3 0.8 %copy-start.1 = (bf16[256,768]{1,0:T(8,128)(2,1)}, bf16[256,768]{1,0:T(8,128)(2,1)S(1)}, u32[]{:S(2)}) copy-start(bf16[256,768]{1,0:T(8,128)(2,1)S(1)} %collective-permute-done.refs_7_) | copy-start | bytes 1179652
  33.1 6.3 %collective-permute-start.2 = (bf16[256,384]{1,0:T(8,128)(2,1)}, bf16[256,384]{1,0:T(8,128)(2,1)S(1)}, u32[]{:S(2)}, u32[]{:S(2)}) collective-permute-start(bf16[256,384]{1,0:T(8,128)(2,1)} %get-tuple-element.32), channel_id=1, source_target_pairs={{8,0},{16,8},{24,16},{0,24},{9,1},{17,9},{25,17},{1,25},{10,2},{18... | collective-permute-start | bytes 589832 | tf_op jit(solution)/shard_map/ppermute | solution.py:28
  39.3 0.7 copy-start
where the time goes:
time: 74 us; the launch traced here: 73.5 us
  Pallas kernels  65 us (88%)
  starting transfers between devices  5.98 us (8%)
  local copies, waits for them, and re-layouts  1.48 us (2%)
    pallas_call x3, Pallas kernels, attention(): pl.pallas_call(functools.partial(attention_kernel, start is not None, pri...  24.1 us
    pallas_call x1, Pallas kernels, reduced(): pl.pallas_call(functools.partial(reduce_kernel, seqs, planes), in_specs=[...  22.5 us
    pallas_call x1, Pallas kernels, epilogue(): pl.pallas_call(functools.partial(epilogue_kernel, counts), grid_spec=pltp...  8.72 us
    pallas_call x1, Pallas kernels, prologue(): pl.pallas_call(prologue_kernel, grid_spec=pltpu.PrefetchScalarGridSpec(nu...  7.47 us
    ppermute x3, starting transfers between devices, from_behind(): return lax.ppermute(block, axis, route)  5.98 us
    pallas_call x1, Pallas kernels, finished(): pl.pallas_call(functools.partial(finish_kernel, limit), in_specs=[vmem],...  2.18 us
  transfers between devices with their start and end apart: 3, of which 1 were waited for; matrix products, arithmetic and copies ran while one was open for 0% of the time, Pallas kernels for 25%

commit v1 on v0

v1 whole, which is shorter than its diff:
```python
import functools
import math

import jax
import jax.numpy as jnp
from jax import lax
from jax.experimental import pallas as pl
from jax.experimental.pallas import tpu as pltpu
from jax.sharding import PartitionSpec as P

HEAD_SIZE = 128
CORES = 2
LANES = 128
TOGETHER = 2
CHUNKS = 4

EPS = 1e-05
ADAPTER_SCALE = 2.0
F32 = jnp.float32
BF16 = jnp.bfloat16
NT = (((1,), (1,)), ((), ()))
NN = (((1,), (0,)), ((), ()))
MESH = pl.DeviceIdType.MESH


def dot(left, right, dims):
    return lax.dot_general(left, right, dims, preferred_element_type=F32)


def stack(pieces):
    return jnp.concatenate(pieces, axis=0)


def beside(pieces):
    return jnp.concatenate(pieces, axis=1)


def split(value):
    high = value.astype(BF16)
    return high, (value - high.astype(F32)).astype(BF16)


def fused_kernel(
    seqs,
    planes,
    heads_ref,
    x_hbm,
    fq_hbm,
    grad_hbm,
    key_hbm,
    fv_hbm,
    scale_hbm,
    qdown_hbm,
    vdown_hbm,
    qup_hbm,
    vup_hbm,
    full_e,
    full_q,
    full_v,
    x,
    fq,
    grad,
    key,
    fv,
    scale,
    qdown,
    vdown,
    qup,
    vup,
    value,
    key_out,
    value_out,
    mid_out,
    key_in,
    value_in,
    mid_in,
    hand_out,
    hand_in,
    part_e,
    part_q,
    part_v,
    parts_e,
    parts_q,
    parts_v,
    column_e,
    column_q,
    column_v,
    sem_load,
    sem_pass_send,
    sem_pass_recv,
    sem_send,
    sem_recv,
    query_mid,
    query_mid_t,
    total_q,
    total_v,
    dvalue,
    keys_t,
    tiles,
):
    rows, width = x.shape
    rank = qdown.shape[0]
    kv, _, wide = fq.shape
    half = kv // 2
    per = wide // HEAD_SIZE
    queries = kv * wide
    factor = 1.0 / math.sqrt(HEAD_SIZE)
    group = seqs * CORES
    seq = lax.axis_index("seq")
    place = lax.axis_index("dp")
    plane = place // CORES
    me = seq * CORES + place % CORES
    parity = lax.rem(seq, 2)
    following = {"seq": lax.rem(seq + 1, seqs)}
    previous = {"seq": lax.rem(seq + seqs - 1, seqs)}

    def in_group(k):
        peer = lax.rem(me + k, group)
        return peer, {"seq": peer // CORES, "dp": plane * CORES + peer % CORES}

    def in_column(k):
        return {"dp": lax.rem(plane + k, planes) * CORES + place % CORES}

    loads = []

    def load(source, target):
        copy = pltpu.make_async_copy(source, target, sem_load.at[len(loads)])
        copy.start()
        loads.append(copy)
        return copy

    def by_head(source, target):
        size = target.shape[2]
        return [load(source.at[:, h * size : (h + 1) * size], target.at[h]) for h in range(kv)]

    block = width // CHUNKS
    get_key = by_head(key_hbm, key)
    get_small = [
        load(s, t) for s, t in ((scale_hbm, scale), (qdown_hbm, qdown), (vdown_hbm, vdown))
    ]
    get_x = [
        load(x_hbm.at[:, c * block : (c + 1) * block], x.at[:, c * block : (c + 1) * block])
        for c in range(CHUNKS)
    ]
    get_value = by_head(fv_hbm, fv) + by_head(vup_hbm, vup) + by_head(qup_hbm, qup)
    get_wide = by_head(fq_hbm, fq) + by_head(grad_hbm, grad)

    barrier = pltpu.get_barrier_semaphore()
    for k in range(1, group):
        pl.semaphore_signal(barrier, inc=1, device_id=in_group(k)[1], device_id_type=MESH)
    for k in range(1, planes):
        pl.semaphore_signal(barrier, inc=1, device_id=in_column(k), device_id_type=MESH)

    def remote(source, target, send, recv, device):
        copy = pltpu.make_async_remote_copy(
            src_ref=source,
            dst_ref=target,
            send_sem=send,
            recv_sem=recv,
            device_id=device,
            device_id_type=MESH,
        )
        copy.start()
        return copy

    passed = []

    def hand(source, target, device):
        i = len(passed)
        copy = remote(source, target, sem_pass_send.at[i], sem_pass_recv.at[i], device)
        passed.append(copy)
        return copy

    own_at = lambda i: (1 - parity) * half + i
    prior_at = lambda i: parity * half + i

    for copy in get_key:
        copy.wait()
    for i in range(half):
        key_out[i] = key[heads_ref[own_at(i)]]
    for copy in get_small:
        copy.wait()
    folded = []
    for i in range(width // LANES):
        cols = slice(i * LANES, (i + 1) * LANES)
        down = stack([qdown[:, cols].astype(F32), vdown[:, cols].astype(F32)])
        folded.append(stack(split(down * scale[i : i + 1, :].astype(F32))))

    squares = jnp.zeros((rows, LANES), F32)
    mids = jnp.zeros((rows, 4 * rank), F32)
    for c in range(CHUNKS):
        get_x[c].wait()
        each = block // LANES
        piece = x[:, c * block : (c + 1) * block]
        for b in range(each):
            part = piece[:, b * LANES : (b + 1) * LANES].astype(F32)
            squares = squares + part * part
        folds = beside(folded[c * each : (c + 1) * each])
        mids = mids + stack(
            [dot(piece[r * rows // 2 : (r + 1) * rows // 2], folds, NT) for r in range(2)]
        )
        if c == 0:
            pl.semaphore_wait(barrier, group + planes - 2)
            pass_key = [hand(key_out.at[i], key_in.at[i], following) for i in range(half)]
    inverse = lax.rsqrt(jnp.sum(squares, axis=1, keepdims=True) * (1.0 / width) + EPS)
    inverse_row = jnp.broadcast_to(inverse, (rows, LANES)).T[:rank]
    mids = ((mids[:, : 2 * rank] + mids[:, 2 * rank :]) * inverse).astype(BF16)
    twice = (mids * ADAPTER_SCALE).astype(BF16)
    query_mid[...] = twice[:, :rank]
    value_mid = twice[:, rank:]
    eye_r = lax.broadcasted_iota(jnp.int32, (2 * rank, 2 * rank), 0)
    eye_c = lax.broadcasted_iota(jnp.int32, (2 * rank, 2 * rank), 1)
    eye = jnp.where(eye_r == eye_c, ADAPTER_SCALE, 0.0).astype(BF16)
    mids_t = dot(eye, mids, NT)
    query_mid_t[...] = mids_t[:rank].astype(BF16)
    mid_out[...] = mids_t[rank:].astype(BF16)
    for copy in get_value:
        copy.wait()
    for h in range(kv):
        value[h] = (fv[h].astype(F32) + dot(value_mid, vup[h], NN)).astype(BF16)
    for i in range(half):
        value_out[i] = value[heads_ref[own_at(i)]]
    pass_mid = hand(mid_out, mid_in, following)
    pass_value = [hand(value_out.at[i], value_in.at[i], following) for i in range(half)]
    for copy in get_wide:
        copy.wait()

    together = TOGETHER
    groups = per // together
    part_rows = rows // 2
    span = together * part_rows
    log2e = factor * math.log2(math.e)
    scores_at, dprob_at, weights_at, dscore_at = tiles
    total_q[...] = jnp.zeros_like(total_q)
    total_v[...] = jnp.zeros_like(total_v)
    hand_out[...] = jnp.zeros_like(hand_out)
    used = queries + kv * HEAD_SIZE
    if used < part_e.shape[1]:
        part_e[:, used:] = jnp.zeros((rank, part_e.shape[1] - used), BF16)

    def piled(array):
        return stack([array[:, k * HEAD_SIZE : (k + 1) * HEAD_SIZE] for k in range(together)])

    def phase(with_prior):
        before = rows if with_prior else 0
        reaches = [before + part_rows, before + rows]
        place_of = prior_at if with_prior else own_at

        def both(i, head, mine, given):
            return stack([given[i], mine[head]]) if with_prior else mine[head]

        def opened(i, p):
            slot = p % 2
            head = heads_ref[place_of(i)]
            cols = slice(p * together * HEAD_SIZE, (p + 1) * together * HEAD_SIZE)
            keys = both(i, head, key, key_in)
            values = both(i, head, value, value_in)
            for a in range(2):
                at = slice(a * part_rows, (a + 1) * part_rows)
                reach = reaches[a]
                adapted = dot(query_mid[at, :], qup[head, :, cols], NN)
                query = (fq[head, at, cols].astype(F32) + adapted).astype(BF16)
                scores_at[slot][a][:reach, :] = dot(keys[:reach], piled(query), NT)
                dprob_at[slot][a][:reach, :] = dot(values[:reach], piled(grad[head, at, cols]), NT)

        def weighed(p):
            slot = p % 2
            key_pos = lax.broadcasted_iota(jnp.int32, (part_rows, span), 0)
            query_pos = lax.broadcasted_iota(jnp.int32, (part_rows, span), 1)
            causal = key_pos <= lax.rem(query_pos, part_rows)
            for a in range(2):
                reach = reaches[a]
                free = reach - part_rows
                scores = scores_at[slot][a][:reach, :]
                dprob = dprob_at[slot][a][:reach, :]
                diagonal = jnp.where(causal, scores[free:], -jnp.inf)
                scores = stack([scores[:free], diagonal]) if free else diagonal
                top = jnp.max(scores, axis=0, keepdims=True)
                exponent = jnp.exp2((scores - top) * log2e)
                probs = exponent * (1.0 / jnp.sum(exponent, axis=0, keepdims=True))
                weights = probs.astype(BF16)
                weights_at[slot][a][:reach, :] = weights
                delta = jnp.sum(weights.astype(F32) * dprob, axis=0, keepdims=True)
                dscore_at[slot][a][:reach, :] = (probs * (dprob - delta)).astype(BF16)

        def closed(i, p):
            slot = p % 2
            pos = place_of(i)
            head = heads_ref[pos]
            cols = slice(p * together * HEAD_SIZE, (p + 1) * together * HEAD_SIZE)
            terms, dqs = [], []
            for a in range(2):
                at = slice(a * part_rows, (a + 1) * part_rows)
                reach = reaches[a]
                grads = piled(grad[head, at, cols])
                terms.append(dot(weights_at[slot][a][:reach, :], grads, NN))
                dqs.append(dot(keys_t[:, :reach], dscore_at[slot][a][:reach, :], NN).astype(BF16))
            dv = stack([terms[1][: reaches[0]] + terms[0], terms[1][reaches[0] :]])
            if p:
                dv = dv + dvalue[: reaches[1], :]
            dquery = stack(
                [
                    beside([dq[:, k * part_rows : (k + 1) * part_rows] for dq in dqs])
                    for k in range(together)
                ]
            )
            at = pl.multiple_of(pos * wide + p * together * HEAD_SIZE, HEAD_SIZE)
            part_e[:, pl.ds(at, together * HEAD_SIZE)] = (
                dot(query_mid_t[...], dquery, NT) * factor
            ).astype(BF16)
            total_q[...] += dot(qup[head, :, cols], dquery, NN)
            if p < groups - 1:
                dvalue[: reaches[1], :] = dv
                return
            up = vup[head]
            mine = dv[before:].astype(BF16)
            raw = dot(mid_out[...], mine, NN)
            total_v[...] += dot(up, mine, NT)
            if before:
                others = dv[:before].astype(BF16)
                raw = raw + dot(mid_in[...], others, NN)
                hand_out[...] += dot(up, others, NT)
            at = pl.multiple_of(queries + pos * HEAD_SIZE, HEAD_SIZE)
            part_e[:, pl.ds(at, HEAD_SIZE)] = raw.astype(BF16)

        def arrived(i):
            for source, target, first in ((key_out, key_in, 0), (value_out, value_in, half + 1)):
                pltpu.make_async_remote_copy(
                    src_ref=source.at[i],
                    dst_ref=target.at[i],
                    send_sem=sem_pass_send.at[first + i],
                    recv_sem=sem_pass_recv.at[first + i],
                    device_id=following,
                    device_id_type=MESH,
                ).wait_recv()

        def transposed(i):
            keys_t[:, : reaches[1]] = both(i, heads_ref[place_of(i)], key, key_in).T

        if with_prior:
            pass_mid.wait_recv()
            arrived(0)
        last = (groups - 1) % 2
        for a in range(2):
            weights_at[last][a][...] = jnp.zeros_like(weights_at[last][a])
            dscore_at[last][a][...] = jnp.zeros_like(dscore_at[last][a])
        dvalue[...] = jnp.zeros_like(dvalue)
        transposed(0)
        opened(0, 0)

        def body(i, carry):
            later = lax.rem(i + 1, half)
            if with_prior:

                @pl.when(i < half - 1)
                def _():
                    arrived(i + 1)

            for p in range(groups):
                if p + 1 < groups:
                    opened(i, p + 1)
                else:
                    opened(later, 0)
                weighed(p)
                if p:
                    closed(i, p - 1)
                else:
                    closed(lax.rem(i + half - 1, half), groups - 1)
                    transposed(i)
            return carry

        lax.fori_loop(0, half, body, 0)
        closed(half - 1, groups - 1)

    phase(False)
    phase(True)
    pass_hand = hand(hand_out, hand_in, previous)

    sums = {
        "e": (part_e, parts_e, column_e, full_e, 0),
        "q": (part_q, parts_q, column_q, full_q, 1),
        "v": (part_v, parts_v, column_v, full_v, 2),
    }
    steps = 2 * (group - 1) + planes - 1
    sent = {name: [[], [], []] for name in sums}

    def share(array, index):
        piece = array.shape[1] // group
        return array.at[:, pl.ds(pl.multiple_of(index * piece, piece), piece)]

    def scatter(name):
        source, parts, _, _, base = sums[name]
        for k in range(1, group):
            peer, device = in_group(k)
            at = base * steps + k - 1
            sent[name][0].append(
                remote(
                    share(source, peer), parts.at[k - 1], sem_send.at[at], sem_recv.at[at], device
                )
            )

    def across(name):
        source, parts, column, _, base = sums[name]
        amount = share(source, me)[...].astype(F32)
        for k in range(1, group):
            sent[name][0][k - 1].wait_recv()
            amount = amount + parts[k - 1].astype(F32)
        column[plane] = amount.astype(BF16)
        for k in range(1, planes):
            at = base * steps + group - 1 + k - 1
            sent[name][1].append(
                remote(
                    column.at[plane],
                    column.at[plane],
                    sem_send.at[at],
                    sem_recv.at[at],
                    in_column(k),
                )
            )

    def gather(name):
        _, _, column, full, base = sums[name]
        for copy in sent[name][1]:
            copy.wait_recv()
        amount = column[0].astype(F32)
        for i in range(1, planes):
            amount = amount + column[i].astype(F32)
        share(full, me)[...] = amount.astype(BF16)
        for k in range(1, group):
            at = base * steps + group + planes - 2 + k - 1
            sent[name][2].append(
                remote(
                    share(full, me),
                    share(full, me),
                    sem_send.at[at],
                    sem_recv.at[at],
                    in_group(k)[1],
                )
            )

    def spread(amount, target):
        inner = (amount * ADAPTER_SCALE).astype(BF16).astype(F32) * inverse_row
        inner = stack(split(inner))
        for c in range(8):
            cols = slice(c * width // 8, (c + 1) * width // 8)
            out = dot(inner, x[:, cols], NN)
            target[:, cols] = (out[:rank] + out[rank:]).astype(BF16)

    scatter("e")
    spread(total_q[...] * factor, part_q)
    scatter("q")
    pass_hand.wait_recv()
    spread(total_v[...] + hand_in[...], part_v)
    scatter("v")
    for step in (across, gather):
        for name in sums:
            step(name)
    for name in sums:
        for copy in sent[name][2]:
            copy.wait_recv()
    for copy in passed:
        copy.wait_send()
    for name in sums:
        for copies in sent[name]:
            for copy in copies:
                copy.wait_send()


def fused(heads, x, fq, grads, keys, values, scale, qdown, vdown, qup, vup, seqs, planes):
    rows, width = x.shape
    rank = qdown.shape[0]
    half = heads.shape[0] // 2
    group = seqs * CORES
    kv = heads.shape[0]
    used = fq.shape[1] + keys.shape[1]
    unit = group * LANES
    narrow = -(-used // unit) * unit
    operands = (x, fq, grads, keys, values, scale, qdown, vdown, qup, vup)
    vmem = pl.BlockSpec(memory_space=pltpu.VMEM)
    dma = pltpu.SemaphoreType.DMA
    sizes = (narrow, width, width)
    passes = 2 * half + 2
    steps = 3 * (2 * (group - 1) + planes - 1)
    blocks = lambda count: pltpu.VMEM((count, rows, HEAD_SIZE), BF16)
    tile = lambda kind: tuple(
        pltpu.VMEM((n * rows // 2, TOGETHER * rows // 2), kind) for n in (3, 4)
    )

    def held(a):
        if a.shape[1] == width or a.shape[1] == LANES:
            return pltpu.VMEM(a.shape, a.dtype)
        return pltpu.VMEM((kv, a.shape[0], a.shape[1] // kv), a.dtype)

    return pl.pallas_call(
        functools.partial(fused_kernel, seqs, planes),
        in_specs=[pl.BlockSpec(memory_space=pltpu.SMEM)]
        + [pl.BlockSpec(memory_space=pl.ANY)] * len(operands),
        out_specs=[vmem] * 3,
        out_shape=[jax.ShapeDtypeStruct((rank, n), BF16) for n in sizes],
        scratch_shapes=[held(a) for a in operands]
        + [held(values)]
        + [blocks(half), blocks(half), pltpu.VMEM((rank, rows), BF16)] * 2
        + [pltpu.VMEM((rank, rows), F32)] * 2
        + [pltpu.VMEM((rank, n), BF16) for n in sizes]
        + [pltpu.VMEM((group - 1, rank, n // group), BF16) for n in sizes]
        + [pltpu.VMEM((planes, rank, n // group), BF16) for n in sizes]
        + [dma((4 + 6 * kv + CHUNKS,)), dma((passes,)), dma((passes,))]
        + [dma((steps,)), dma((steps,))]
        + [pltpu.VMEM((rows, rank), BF16), pltpu.VMEM((rank, rows), BF16)]
        + [pltpu.VMEM((rank, rows), F32)] * 2
        + [pltpu.VMEM((2 * rows, HEAD_SIZE), F32), pltpu.VMEM((HEAD_SIZE, 2 * rows), BF16)]
        + [tuple(tuple(tile(t) for _ in range(2)) for t in (F32, F32, BF16, BF16))],
        compiler_params=pltpu.CompilerParams(collective_id=0, has_side_effects=True),
        name="fused",
    )(heads, *operands)


def finish_kernel(
    limit,
    heads_ref,
    full_e,
    full_q,
    full_v,
    scale_ref,
    qdown_ref,
    vdown_ref,
    qa_ref,
    qb_ref,
    va_ref,
    vb_ref,
    gain_ref,
):
    rank, width = qa_ref.shape
    kv = vb_ref.shape[1] // HEAD_SIZE
    wide = qb_ref.shape[1] // kv
    used = qb_ref.shape[1] + vb_ref.shape[1]
    squares = jnp.zeros((rank, LANES), F32)
    tops = jnp.zeros((1, LANES), F32)
    for i in range(width // LANES):
        cols = slice(i * LANES, (i + 1) * LANES)
        scale = scale_ref[i : i + 1, :].astype(F32)
        query, value = full_q[:, cols].astype(F32), full_v[:, cols].astype(F32)
        gain = qdown_ref[:, cols].astype(F32) * query + vdown_ref[:, cols].astype(F32) * value
        gain = jnp.sum(gain, axis=0, keepdims=True)
        query, value = query * scale, value * scale
        squares = squares + query * query + value * value
        tops = tops + gain * gain
        qa_ref[:, cols], va_ref[:, cols] = query, value
        gain_ref[i : i + 1, :] = gain
    for i in range(used // LANES):
        piece = full_e[:, i * LANES : (i + 1) * LANES].astype(F32)
        squares = squares + piece * piece
    squares = jnp.sum(squares, axis=0, keepdims=True) + tops
    squares = jnp.sum(squares, axis=1, keepdims=True)
    scale = jnp.minimum(1.0, limit / jnp.sqrt(squares))
    qa_ref[...] = qa_ref[...] * scale
    va_ref[...] = va_ref[...] * scale
    gain_ref[...] = gain_ref[...] * scale
    for pos in range(kv):
        head = heads_ref[pos]
        at = pl.multiple_of(head * wide, HEAD_SIZE)
        qb_ref[:, pl.ds(at, wide)] = full_e[:, pos * wide : (pos + 1) * wide].astype(F32) * scale
        at = pl.multiple_of(head * HEAD_SIZE, HEAD_SIZE)
        first = kv * wide + pos * HEAD_SIZE
        piece = full_e[:, first : first + HEAD_SIZE].astype(F32)
        vb_ref[:, pl.ds(at, HEAD_SIZE)] = piece * scale


def finished(heads, fulls, scale, qdown, vdown, limit, widths):
    rank, width = qdown.shape
    vmem = pl.BlockSpec(memory_space=pltpu.VMEM)
    return pl.pallas_call(
        functools.partial(finish_kernel, limit),
        in_specs=[pl.BlockSpec(memory_space=pltpu.SMEM)] + [vmem] * 6,
        out_specs=[vmem] * (len(widths) + 1),
        out_shape=[jax.ShapeDtypeStruct((rank, w), F32) for w in widths]
        + [jax.ShapeDtypeStruct((width // LANES, LANES), F32)],
        name="finished",
    )(heads, *fulls, scale, qdown, vdown)


def shards(
    layer_input,
    frozen_queries,
    frozen_keys,
    frozen_values,
    output_gradient,
    norm_scale_vector,
    query_down_weight,
    query_up_weight,
    value_down_weight,
    value_up_weight,
    head_ordering,
):
    seqs = lax.axis_size("seq")
    planes = lax.axis_size("dp") // CORES
    rank, width = query_down_weight.shape
    queries = query_up_weight.shape[1]
    kv = value_up_weight.shape[1]
    scale = norm_scale_vector.reshape(width // LANES, LANES)
    fulls = fused(
        head_ordering,
        layer_input[0],
        frozen_queries[0],
        output_gradient[0],
        frozen_keys[0],
        frozen_values[0],
        scale,
        query_down_weight,
        value_down_weight,
        query_up_weight,
        value_up_weight,
        seqs,
        planes,
    )
    limit = math.sqrt(rank * (2 * width + queries + kv) + width)
    qa, qb, va, vb, gain = finished(
        head_ordering,
        fulls,
        scale,
        query_down_weight,
        value_down_weight,
        limit,
        (width, queries, width, kv),
    )
    return (qa, qb, va, vb, gain.reshape(width))


def solution(mesh):
    placed = (
        P("dp", "seq", None),
        P("dp", "seq", None),
        P("dp", "seq", None),
        P("dp", "seq", None),
        P("dp", "seq", None),
        P(),
        P(),
        P(),
        P(),
        P(),
        P(),
    )
    return jax.shard_map(
        shards, mesh=mesh, in_specs=placed, out_specs=(P(), P(), P(), P(), P()), check_vma=False
    )
```

time: 74 us -> 50.9 us (0.69)
  Pallas kernels: 65 us -> 50 us
  starting transfers between devices: 5.98 us -> 0 us
  local copies, waits for them, and re-layouts: 1.48 us -> 0 us
    pallas_call x7 -> x2, Pallas kernels: 65 us -> 50 us  [the longest x1 47.6 us: fused(): pl.pallas_call(functools.partial(fused_kernel, seqs, planes), in_specs=[p...]
    ppermute x3 -> x0, starting transfers between devices: 5.98 us -> none  [from_behind(): return lax.ppermute(block, axis, route)]
    unnamed x6 -> x0, local copies, waits for them, and re-layouts: 1.48 us -> none
  transfers between devices with their start and end apart: 3 -> 0, of which waited for: 1 -> 0; matrix products, arithmetic and copies ran while one was open for 0% -> 0% of each run, Pallas kernels for 25% -> 0%
where the time goes in v1:
time: 50.9 us; the launch traced here: 50.7 us
  Pallas kernels  50 us (98%)
  between operations  0.64 us (1%)
    pallas_call x1, Pallas kernels, fused(): pl.pallas_call(functools.partial(fused_kernel, seqs, planes), in_specs=[p...  47.6 us
    pallas_call x1, Pallas kernels, finished(): pl.pallas_call(functools.partial(finish_kernel, limit), in_specs=[pl.Bloc...  2.41 us

profile of v1, /device:TPU:0, one launch (start us, length us, event | category | flops | bytes accessed | tf_op | source)
XLA Modules:
  0.0 50.7 jit_solution(10522637257999258757)
XLA Ops:
  0.6 47.6 %fused.1 = (bf16[8,7168]{1,0:T(8,128)(2,1)}, bf16[8,8192]{1,0:T(8,128)(2,1)}, bf16[8,8192]{1,0:T(8,128)(2,1)}) custom-call(s32[6]{0:T(128)} %heads_ref.3, bf16[256,8192]{1,0:T(8,128)(2,1)} %bitcast.7, bf16[256,6144]{1,0:T(8,128)(2,1)} %bitcast.8, bf16[256,6144]{1,0:T(8,128)(2,1)} %bitcast.9, bf16[256,768]{1,0:T(8,128)(2,1)} %bitcast.10, ...), custom_call_target="tpu_custom_call" | custom-call | tf_op jit(solution)/shard_map/fused/pallas_call | solution.py:494
  48.3 2.4 %finished.1 = (f32[8,8192]{1,0:T(8,128)}, f32[8,6144]{1,0:T(8,128)}, f32[8,8192]{1,0:T(8,128)}, f32[8,768]{1,0:T(8,128)}, f32[64,128]{1,0:T(8,128)}) custom-call(s32[6]{0:T(128)} %heads_ref.3, bf16[8,7168]{1,0:T(8,128)(2,1)} %get-tuple-element.13.full_e, bf16[8,8192]{1,0:T(8,128)(2,1)} %get-tuple-element.14.full_q, ...), custom_call_target="tpu_custom_call" | custom-call | tf_op jit(solution)/shard_map/finished/pallas_call | solution.py:572
